TPU v7x, 32 devices: a whole 2x2x4 slice. The times are simulated.
32 devices in a mesh: wide: 8 (over y, x, core), narrow: 4 (over z).
Axes of the slice: x: 2, y: 2, z: 4, core: 2. Of those that a mesh axis runs over, the one named last changes fastest.
Arguments:
- tokens: bfloat16 [128, 512, 768], P(('wide', 'narrow')), may hold values from -6 to 6
- lengths: int32 [128], P(('wide', 'narrow')), may hold values from 128 to 512, as said below
- query_lengths: int32 [128], P(('wide', 'narrow')), may hold values from 2 to 64
- language_ids: int32 [128], P(('wide', 'narrow')), may hold values from 0 to 99
- position_table: bfloat16 [512, 768], P('wide', 'narrow'), may hold values from -3 to 3
- segment_table: bfloat16 [2, 768], replicated, may hold values from -3 to 3
- language_table: bfloat16 [100, 768], replicated, may hold values from -3 to 3
- query_weight: bfloat16 [768, 768], P('wide', 'narrow'), may hold values from -0.21875 to 0.21875
- key_weight: bfloat16 [768, 768], P('wide', 'narrow'), may hold values from -0.21875 to 0.21875
- value_weight: bfloat16 [768, 768], P('wide', 'narrow'), may hold values from -0.21875 to 0.21875
- output_weight: bfloat16 [768, 768], P('wide', 'narrow'), may hold values from -0.875 to 0.875
- query_bias: bfloat16 [768], replicated, may hold values from -2 to 2
- value_bias: bfloat16 [768], replicated, may hold values from -2 to 2
- output_bias: bfloat16 [768], replicated, may hold values from -2 to 2
- first_gain: bfloat16 [768], replicated, may hold values from 0.5 to 1.5
- first_shift: bfloat16 [768], replicated, may hold values from -2 to 2
- up_weight: bfloat16 [768, 3072], P('wide', 'narrow'), may hold values from -0.21875 to 0.21875
- up_bias: bfloat16 [3072], replicated, may hold values from -2 to 2
- down_weight: bfloat16 [3072, 768], P('wide', 'narrow'), may hold values from -0.109375 to 0.109375
- down_bias: bfloat16 [768], replicated, may hold values from -2 to 2
- second_gain: bfloat16 [768], replicated, may hold values from 0.5 to 1.5
- second_shift: bfloat16 [768], replicated, may hold values from -2 to 2
- cotangent: bfloat16 [128, 512, 768], P(('wide', 'narrow')), may hold values from -6 to 6
Outputs:
- layer_out: bfloat16 [128, 512, 768], P(('wide', 'narrow'))
- token_grad: bfloat16 [128, 512, 768], P(('wide', 'narrow'))
- position_grad: float32 [512, 768], P('wide', 'narrow')
- segment_grad: float32 [2, 768], replicated
- language_grad: float32 [100, 768], replicated
- query_weight_grad: float32 [768, 768], P('wide', 'narrow')
- key_weight_grad: float32 [768, 768], P('wide', 'narrow')
- value_weight_grad: float32 [768, 768], P('wide', 'narrow')
- output_weight_grad: float32 [768, 768], P('wide', 'narrow')
- query_bias_grad: float32 [768], replicated
- value_bias_grad: float32 [768], replicated
- output_bias_grad: float32 [768], replicated
- first_gain_grad: float32 [768], replicated
- first_shift_grad: float32 [768], replicated
- up_weight_grad: float32 [768, 3072], P('wide', 'narrow')
- up_bias_grad: float32 [3072], replicated
- down_weight_grad: float32 [3072, 768], P('wide', 'narrow')
- down_bias_grad: float32 [768], replicated
- second_gain_grad: float32 [768], replicated
- second_shift_grad: float32 [768], replicated
Inputs may be any that keep to these rules, and one draw needn't show every extreme that they name: Each pair has lengths live tokens, the rest are padding; some pair fills all 512 positions. `query_lengths`: A pair's queries lie within its live tokens.
All inputs are finite; a program needn't handle non-finite values.
Results may differ from a plain program's by a relative error of at most 0.015.
The roundings to bfloat16 on the way count: a program that leaves them out, or rounds other values in their place, can miss the bound.
Values may be sent and summed in bfloat16 or wider, within the bound.
No kernel may reach another device: no remote copies, remote signals or barrier semaphores. Data moves between devices by JAX's collectives and lax.ppermute only.
A program may use at most 256 MiB of HBM per device.

v0:
```python
import math
import jax
import jax.numpy as jnp
from jax import lax
from jax.sharding import PartitionSpec as P

H = 12
HD = 64
EPSILON = 1e-05


def normalize(inputs, scales, offset):
    average = jnp.mean(inputs, axis=-1, keepdims=True)
    centered = inputs - average
    spread = jnp.mean(centered * centered, axis=-1, keepdims=True)
    return centered * lax.rsqrt(spread + EPSILON) * scales + offset


def matmul(left_side, right_side):
    return jnp.dot(left_side, right_side, preferred_element_type=jnp.float32)


def matmul_first_t(left_side, right_side):
    return lax.dot_general(
        left_side, right_side, (((0,), (0,)), ((), ())), preferred_element_type=jnp.float32
    )


def matmul_second_t(left_side, right_side):
    return lax.dot_general(
        left_side, right_side, (((1,), (1,)), ((), ())), preferred_element_type=jnp.float32
    )


def exact_gelu(inputs):
    return jax.nn.gelu(inputs, approximate=False)


def split_heads(flattened, seq_count, seq_len):
    return (
        flattened.reshape(seq_count, seq_len, H, HD)
        .transpose(0, 2, 1, 3)
        .reshape(seq_count * H, seq_len, HD)
    )


def join_heads(blocks, seq_count, seq_len):
    return (
        blocks.reshape(seq_count, H, seq_len, HD)
        .transpose(0, 2, 1, 3)
        .reshape(seq_count * seq_len, H * HD)
    )


def assemble(stacked, wide_count, narrow_count):
    block_rows = stacked.shape[1]
    block_cols = stacked.shape[2]
    return (
        stacked.reshape(wide_count, narrow_count, block_rows, block_cols)
        .transpose(0, 2, 1, 3)
        .reshape(wide_count * block_rows, narrow_count * block_cols)
    )


def disassemble(whole, wide_count, narrow_count):
    block_rows = whole.shape[0] // wide_count
    block_cols = whole.shape[1] // narrow_count
    return (
        whole.reshape(wide_count, block_rows, narrow_count, block_cols)
        .transpose(0, 2, 1, 3)
        .reshape(wide_count * narrow_count, block_rows, block_cols)
    )


def block_scores(query_rows, key_rows, length):
    factor = 1.0 / math.sqrt(HD)
    products = matmul_second_t(query_rows, key_rows) * factor
    keeping = lax.broadcasted_iota(jnp.int32, products.shape, 1) < length
    return jnp.where(keeping, products, -1e30)


def attend_block(pieces):
    query_rows, key_rows, value_rows, length = pieces
    scores = block_scores(query_rows, key_rows, length)
    row_max = jnp.max(scores, axis=1, keepdims=True)
    weights = jnp.exp(scores - row_max)
    row_total = jnp.sum(weights, axis=1, keepdims=True)
    low_weights = (weights / row_total).astype(jnp.bfloat16)
    context = matmul(low_weights, value_rows)
    return (context, (row_max + jnp.log(row_total))[:, 0])


def attend_back(pieces):
    query_rows, key_rows, value_rows, length, log_totals, grad_context = pieces
    scores = block_scores(query_rows, key_rows, length)
    probabilities = jnp.exp(scores - log_totals[:, None])
    grad_probs = matmul_second_t(grad_context, value_rows)
    row_dots = jnp.sum(probabilities * grad_probs, axis=1, keepdims=True)
    grad_scores = (probabilities * (grad_probs - row_dots)).astype(jnp.bfloat16)
    factor = 1.0 / math.sqrt(HD)
    grad_query = matmul(grad_scores, key_rows) * factor
    grad_key = matmul_first_t(grad_scores, query_rows) * factor
    grad_value = matmul_first_t(probabilities.astype(jnp.bfloat16), grad_context)
    return (grad_query, grad_key, grad_value)


def on_device(
    tokens,
    lengths,
    query_lengths,
    language_ids,
    position_table,
    segment_table,
    language_table,
    query_weight,
    key_weight,
    value_weight,
    output_weight,
    query_bias,
    value_bias,
    output_bias,
    first_gain,
    first_shift,
    up_weight,
    up_bias,
    down_weight,
    down_bias,
    second_gain,
    second_shift,
    cotangent,
):
    seq_count, seq_len, features = tokens.shape
    row_count = seq_count * seq_len
    wide_count = lax.axis_size("wide")
    narrow_count = lax.axis_size("narrow")
    attention_stacks = (
        lax.all_gather(position_table[None], ("wide", "narrow"), axis=0, tiled=True),
        lax.all_gather(query_weight[None], ("wide", "narrow"), axis=0, tiled=True),
        lax.all_gather(key_weight[None], ("wide", "narrow"), axis=0, tiled=True),
        lax.all_gather(value_weight[None], ("wide", "narrow"), axis=0, tiled=True),
        lax.all_gather(output_weight[None], ("wide", "narrow"), axis=0, tiled=True),
    )
    position_full, query_full, key_full, value_full, output_full = [
        assemble(stacked, wide_count, narrow_count) for stacked in attention_stacks
    ]
    feedforward_stacks = (
        lax.all_gather(up_weight[None], ("wide", "narrow"), axis=0, tiled=True),
        lax.all_gather(down_weight[None], ("wide", "narrow"), axis=0, tiled=True),
    )
    up_full, down_full = [
        assemble(stacked, wide_count, narrow_count) for stacked in feedforward_stacks
    ]
    places = lax.broadcasted_iota(jnp.int32, (seq_count, seq_len), 1)
    passage = (places >= query_lengths[:, None])[:, :, None]
    segment_float = segment_table.astype(jnp.float32)
    segment_rows = jnp.where(passage, segment_float[1], segment_float[0])
    language_count = language_table.shape[0]
    language_hot = (
        language_ids[:, None] == lax.broadcasted_iota(jnp.int32, (seq_count, language_count), 1)
    ).astype(jnp.bfloat16)
    language_rows = matmul(language_hot, language_table)
    start = (
        tokens.astype(jnp.float32)
        + position_full.astype(jnp.float32)[None]
        + segment_rows
        + language_rows[:, None, :]
    )
    flattened = start.reshape(row_count, features)
    first_in = flattened.astype(jnp.bfloat16)
    query_rows = (matmul(first_in, query_full) + query_bias.astype(jnp.float32)).astype(
        jnp.bfloat16
    )
    key_rows = matmul(first_in, key_full).astype(jnp.bfloat16)
    value_rows = (matmul(first_in, value_full) + value_bias.astype(jnp.float32)).astype(
        jnp.bfloat16
    )
    query_heads = split_heads(query_rows, seq_count, seq_len)
    key_heads = split_heads(key_rows, seq_count, seq_len)
    value_heads = split_heads(value_rows, seq_count, seq_len)
    head_lengths = jnp.repeat(lengths, H)
    context_blocks, log_totals = lax.map(
        attend_block, (query_heads, key_heads, value_heads, head_lengths)
    )
    context = join_heads(context_blocks, seq_count, seq_len).astype(jnp.bfloat16)
    attended = matmul(context, output_full) + output_bias.astype(jnp.float32)
    first_out, first_pull = jax.vjp(
        normalize,
        flattened + attended,
        first_gain.astype(jnp.float32),
        first_shift.astype(jnp.float32),
    )
    second_in = first_out.astype(jnp.bfloat16)
    hidden_pre = matmul(second_in, up_full) + up_bias.astype(jnp.float32)
    hidden = exact_gelu(hidden_pre).astype(jnp.bfloat16)
    branch = matmul(hidden, down_full) + down_bias.astype(jnp.float32)
    final, second_pull = jax.vjp(
        normalize,
        first_out + branch,
        second_gain.astype(jnp.float32),
        second_shift.astype(jnp.float32),
    )
    layer_out = final.astype(jnp.bfloat16).reshape(seq_count, seq_len, features)
    feedforward_again = (
        lax.all_gather(up_weight[None], ("wide", "narrow"), axis=0, tiled=True),
        lax.all_gather(down_weight[None], ("wide", "narrow"), axis=0, tiled=True),
    )
    back_up, back_down = [
        assemble(stacked, wide_count, narrow_count) for stacked in feedforward_again
    ]
    attention_again = (
        lax.all_gather(query_weight[None], ("wide", "narrow"), axis=0, tiled=True),
        lax.all_gather(key_weight[None], ("wide", "narrow"), axis=0, tiled=True),
        lax.all_gather(value_weight[None], ("wide", "narrow"), axis=0, tiled=True),
        lax.all_gather(output_weight[None], ("wide", "narrow"), axis=0, tiled=True),
    )
    back_query, back_key, back_value, back_output = [
        assemble(stacked, wide_count, narrow_count) for stacked in attention_again
    ]
    grad_second, second_gain_grad, second_shift_grad = second_pull(
        cotangent.astype(jnp.float32).reshape(row_count, features)
    )
    grad_branch = grad_second.astype(jnp.bfloat16)
    down_bias_grad = jnp.sum(grad_branch.astype(jnp.float32), axis=0)
    down_weight_grad = matmul_first_t(hidden, grad_branch)
    gelu_value, gelu_pull = jax.vjp(exact_gelu, hidden_pre)
    grad_hidden = gelu_pull(matmul_second_t(grad_branch, back_down))[0].astype(jnp.bfloat16)
    up_bias_grad = jnp.sum(grad_hidden.astype(jnp.float32), axis=0)
    up_weight_grad = matmul_first_t(second_in, grad_hidden)
    grad_first_out = grad_second + matmul_second_t(grad_hidden, back_up)
    grad_first, first_gain_grad, first_shift_grad = first_pull(grad_first_out)
    grad_attended = grad_first.astype(jnp.bfloat16)
    output_bias_grad = jnp.sum(grad_attended.astype(jnp.float32), axis=0)
    output_weight_grad = matmul_first_t(context, grad_attended)
    grad_context = matmul_second_t(grad_attended, back_output).astype(jnp.bfloat16)
    grad_query_blocks, grad_key_blocks, grad_value_blocks = lax.map(
        attend_back,
        (
            query_heads,
            key_heads,
            value_heads,
            head_lengths,
            log_totals,
            split_heads(grad_context, seq_count, seq_len),
        ),
    )
    grad_query = join_heads(grad_query_blocks, seq_count, seq_len).astype(jnp.bfloat16)
    grad_key = join_heads(grad_key_blocks, seq_count, seq_len).astype(jnp.bfloat16)
    grad_value = join_heads(grad_value_blocks, seq_count, seq_len).astype(jnp.bfloat16)
    query_bias_grad = jnp.sum(grad_query.astype(jnp.float32), axis=0)
    value_bias_grad = jnp.sum(grad_value.astype(jnp.float32), axis=0)
    query_weight_grad = matmul_first_t(first_in, grad_query)
    key_weight_grad = matmul_first_t(first_in, grad_key)
    value_weight_grad = matmul_first_t(first_in, grad_value)
    grad_start = (
        grad_first
        + matmul_second_t(grad_query, back_query)
        + matmul_second_t(grad_key, back_key)
        + matmul_second_t(grad_value, back_value)
    )
    token_grad = grad_start.astype(jnp.bfloat16).reshape(seq_count, seq_len, features)
    grad_start_pairs = grad_start.reshape(seq_count, seq_len, features)
    position_local = jnp.sum(grad_start_pairs, axis=0)
    segment_local = jnp.stack(
        [
            jnp.sum(jnp.where(passage, 0.0, grad_start_pairs), axis=(0, 1)),
            jnp.sum(jnp.where(passage, grad_start_pairs, 0.0), axis=(0, 1)),
        ]
    )
    language_local = lax.dot_general(
        language_hot.astype(jnp.float32),
        jnp.sum(grad_start_pairs, axis=1),
        (((0,), (0,)), ((), ())),
        precision=lax.Precision.HIGHEST,
    )
    attention_blocks = (
        lax.psum_scatter(
            disassemble(position_local, wide_count, narrow_count),
            ("wide", "narrow"),
            scatter_dimension=0,
            tiled=True,
        ),
        lax.psum_scatter(
            disassemble(query_weight_grad, wide_count, narrow_count),
            ("wide", "narrow"),
            scatter_dimension=0,
            tiled=True,
        ),
        lax.psum_scatter(
            disassemble(key_weight_grad, wide_count, narrow_count),
            ("wide", "narrow"),
            scatter_dimension=0,
            tiled=True,
        ),
        lax.psum_scatter(
            disassemble(value_weight_grad, wide_count, narrow_count),
            ("wide", "narrow"),
            scatter_dimension=0,
            tiled=True,
        ),
        lax.psum_scatter(
            disassemble(output_weight_grad, wide_count, narrow_count),
            ("wide", "narrow"),
            scatter_dimension=0,
            tiled=True,
        ),
    )
    attention_sums = [summed_block[0] for summed_block in attention_blocks]
    feedforward_blocks = (
        lax.psum_scatter(
            disassemble(up_weight_grad, wide_count, narrow_count),
            ("wide", "narrow"),
            scatter_dimension=0,
            tiled=True,
        ),
        lax.psum_scatter(
            disassemble(down_weight_grad, wide_count, narrow_count),
            ("wide", "narrow"),
            scatter_dimension=0,
            tiled=True,
        ),
    )
    feedforward_sums = [summed_block[0] for summed_block in feedforward_blocks]
    small_sums = lax.psum(
        (
            segment_local,
            language_local,
            query_bias_grad,
            value_bias_grad,
            output_bias_grad,
            first_gain_grad,
            first_shift_grad,
            up_bias_grad,
            down_bias_grad,
            second_gain_grad,
            second_shift_grad,
        ),
        ("wide", "narrow"),
    )
    return (
        layer_out,
        token_grad,
        attention_sums[0],
        small_sums[0],
        small_sums[1],
        attention_sums[1],
        attention_sums[2],
        attention_sums[3],
        attention_sums[4],
        small_sums[2],
        small_sums[3],
        small_sums[4],
        small_sums[5],
        small_sums[6],
        feedforward_sums[0],
        small_sums[7],
        feedforward_sums[1],
        small_sums[8],
        small_sums[9],
        small_sums[10],
    )


def solution(mesh):
    return jax.shard_map(
        on_device,
        mesh=mesh,
        in_specs=(
            P(("wide", "narrow"), None, None),
            P(("wide", "narrow")),
            P(("wide", "narrow")),
            P(("wide", "narrow")),
            P("wide", "narrow"),
            P(),
            P(),
            P("wide", "narrow"),
            P("wide", "narrow"),
            P("wide", "narrow"),
            P("wide", "narrow"),
            P(),
            P(),
            P(),
            P(),
            P(),
            P("wide", "narrow"),
            P(),
            P("wide", "narrow"),
            P(),
            P(),
            P(),
            P(("wide", "narrow"), None, None),
        ),
        out_specs=(
            P(("wide", "narrow"), None, None),
            P(("wide", "narrow"), None, None),
            P("wide", "narrow"),
            P(),
            P(),
            P("wide", "narrow"),
            P("wide", "narrow"),
            P("wide", "narrow"),
            P("wide", "narrow"),
            P(),
            P(),
            P(),
            P(),
            P(),
            P("wide", "narrow"),
            P(),
            P("wide", "narrow"),
            P(),
            P(),
            P(),
        ),
        check_vma=False,
    )
```

profile of v0, /device:TPU:0, one launch (start us, length us, event | category | flops | bytes accessed | tf_op | source)
XLA Modules:
  0.0 2180.7 jit_solution(14981579719575982084)
XLA Ops:
  12.8 79.9 %all-gather = bf16[2048,192]{1,0:T(8,128)(2,1)S(1)} all-gather(bf16[64,192]{1,0:T(8,128)(2,1)} %param.31), channel_id=2, replica_groups=mesh['wide'=8,'narrow'=4] {'wide','narrow'}, dimensions={0}, use_global_device_ids=true | all-gather | bytes 811008 | tf_op jit(solution)/shard_map/all_gather | solution.py:137
  98.9 6.5 fusion.60
  109.7 6.2 add_convert_fusion.3
  123.1 7.7 copy.107
  135.2 6.2 add_convert_fusion.2
  148.6 7.7 copy.109
  156.3 27.0 %all-gather.16.cloned.1.call-done = bf16[3072,192]{1,0:T(8,128)(2,1)} async-done(((bf16[96,192]{1,0:T(8,128)(2,1)}), bf16[3072,192]{1,0:T(8,128)(2,1)}) %all-gather.16.cloned.1.call-update) | async-done | bytes 1179664 | tf_op jit(solution)/shard_map/all_gather | solution.py:139
  187.9 6.2 convolution_convert_fusion.1
  201.2 7.7 copy.108
  209.3 255.0 %while.26 = (s32[]{:T(128)}, bf16[48,512,64]{1,2,0:T(8,128)(2,1)S(1)}, f32[48,512]{1,0:T(8,128)}, s32[48]{0:T(128)S(1)}, bf16[48,512,64]{2,1,0:T(8,128)(2,1)}, /...) while((s32[]{:T(128)}, bf16[48,512,64]{1,2,0:T(8,128)(2,1)S(1)}, ...), condition=%wide.region_3.4_spmd, body=%wide.region_0.3_spmd.sunk | while | flops 69206016 | bytes 3693681 | solution.py:181
  473.0 7.5 fusion.69
  484.2 6.0 copy.87
  493.4 8.2 reshape.353
  509.4 68.8 %multiply_convert_fusion.1 = (bf16[2048,3072]{1,0:T(8,128)(2,1)}, f32[2048,3072]{1,0:T(8,128)}, f32[2048,3072]{1,0:T(8,128)}) fusion(f32[3072]{0:T(1024)S(1)} %convert_element_type.206, bf16[768,3072]{1,0:T(8,128)(2,1)S(1)} %bitcast.362, f32[2048,768]{1,0:T(8,128)S(1)} %bitcast.331, f32[768]{0:T(1024)S(1)} %convert_element_type.204, ...), kind=kOutput, calls=%fused_computation.60 | convolution fusion | flops 10086776832 | bytes 73959424 | tf_op jit(solution)/shard_map/dot_general | solution.py:20
  578.2 15.1 fusion.70
  598.3 4.3 fusion.66
  606.4 29.2 %convert_reduce_fusion = (f32[3072]{0:T(1024)}, bf16[2048,3072]{1,0:T(8,128)(2,1)}) fusion(f32[2048,3072]{1,0:T(8,128)} %get-tuple-element.196, bf16[2048,768]{1,0:T(8,128)(2,1)S(1)} %get-tuple-element.188, bf16[3072,768]{0,1:T(8,128)(2,1)} %bitcast.364, f32[2048,3072]{1,0:T(8,128)} %get-tuple-element.209, f32[3072]{0:T(1024)S(1)} %convert_element_type.206), kind=kOutput, calls=%fused_computation.58 | convolution fusion | flops 9770628096 | bytes 70803456 | tf_op jit(solution)/shard_map/dot_general | solution.py:30
  635.7 19.3 multiply_reduce_fusion.1
  655.0 4.2 fusion.65
  661.3 3.9 convolution_convert_fusion
  675.5 7.7 copy.112
  687.6 467.8 %while.27 = (s32[]{:T(128)}, bf16[48,512,64]{1,2,0:T(8,128)(2,1)S(1)}, bf16[48,512,64]{1,2,0:T(8,128)(2,1)}, bf16[48,512,64]{1,2,0:T(8,128)(2,1)}, s32[48]{0:T(1...) while((s32[]{:T(128)}, ...), condition=%wide.region_14.15_spmd, body=%wide.region_12.14_spmd.sunk | while | flops 170196992 | bytes 9191553 | solution.py:235
  1159.0 4.6 fusion.71
  1167.2 5.0 fusion.72
  1172.2 4.4 copy.97
  1177.7 9.6 select_reduce_fusion.1
  1191.5 8.0 fusion.76
  1199.6 4.6 reduce_sum.251
  1211.3 4.7 bitcast_convert_fusion
  1216.0 4.7 copy.99
  1220.7 8.0 fusion.73
  1228.8 7.9 fusion.74
  1236.8 8.0 fusion.75
  1244.8 16.4 fusion.77
  1261.3 5.9 copy.121
  1267.2 5.3 copy.103
  1273.2 18.6 fusion.61
  1291.8 12.7 reshape.367
  1304.5 9.0 copy.101
  1319.5 5.2 convert_reduce_fusion.4
  1324.9 40.7 %all-reduce = (f32[2,768]{1,0:T(2,128)}, f32[768]{0:T(1024)}, f32[768]{0:T(1024)}, f32[768]{0:T(1024)}, f32[768]{0:T(1024)}, /*index=5*/f32[768]{0:T(1024)}, f32...) all-reduce(f32[2,768]{1,0:T(2,128)S(1)} %pad_maximum_fusion, ...), channel_id=1, replica_groups=mesh['wide'=8,'narrow'=4] {'wide','narrow'}, use_global_device_ids=true, to_apply=%region_19.20 | all-reduce | flops 10752 | bytes 86016 | tf_op jit(solution)/shard_map/psum | solution.py:323
  1365.6 61.2 %reduce-scatter.16.cloned.1.call-done = f32[1,96,192]{2,1,0:T(8,128)} async-done(((f32[32,96,192]{2,1,0:T(8,128)}), f32[1,96,192]{2,1,0:T(8,128)}) %reduce-scatter.16.cloned.1.call-update) | async-done | bytes 73744 | tf_op jit(solution)/shard_map/reduce_scatter | solution.py:300
  1426.8 142.0 %reduce-scatter.8.cloned.1.call-done = f32[1,64,192]{2,1,0:T(8,128)} async-done(((f32[32,64,192]{2,1,0:T(8,128)}), f32[1,64,192]{2,1,0:T(8,128)}) %reduce-scatter.8.cloned.1.call-update) | async-done | bytes 49168 | tf_op jit(solution)/shard_map/reduce_scatter | solution.py:276
  1568.8 105.7 %reduce-scatter.10.cloned.1.call-done = f32[1,96,192]{2,1,0:T(8,128)} async-done(((f32[32,96,192]{2,1,0:T(8,128)}), f32[1,96,192]{2,1,0:T(8,128)}) %reduce-scatter.10.cloned.1.call-update) | async-done | bytes 73744 | tf_op jit(solution)/shard_map/reduce_scatter | solution.py:282
  1674.4 107.2 %reduce-scatter.12.cloned.1.call-done = f32[1,96,192]{2,1,0:T(8,128)} async-done(((f32[32,96,192]{2,1,0:T(8,128)}), f32[1,96,192]{2,1,0:T(8,128)}) %reduce-scatter.12.cloned.1.call-update) | async-done | bytes 73744 | tf_op jit(solution)/shard_map/reduce_scatter | solution.py:288
  1781.7 107.1 %reduce-scatter.14.cloned.1.call-done = f32[1,96,192]{2,1,0:T(8,128)} async-done(((f32[32,96,192]{2,1,0:T(8,128)}), f32[1,96,192]{2,1,0:T(8,128)}) %reduce-scatter.14.cloned.1.call-update) | async-done | bytes 73744 | tf_op jit(solution)/shard_map/reduce_scatter | solution.py:294
  1888.7 141.7 %reduce-scatter.20.cloned.1.call-done = f32[1,384,192]{1,2,0:T(8,128)} async-done(((f32[32,384,192]{1,2,0:T(8,128)}), f32[1,384,192]{1,2,0:T(8,128)}) %reduce-scatter.20.cloned.1.call-update) | async-done | bytes 294928 | tf_op jit(solution)/shard_map/reduce_scatter | solution.py:315
  2030.4 141.5 %reduce-scatter.18.cloned.1.call-done = f32[1,96,768]{2,1,0:T(8,128)} async-done(((f32[32,96,768]{2,1,0:T(8,128)}), f32[1,96,768]{2,1,0:T(8,128)}) %reduce-scatter.18.cloned.1.call-update) | async-done | bytes 294928 | tf_op jit(solution)/shard_map/reduce_scatter | solution.py:309
  (985 shorter events, 843.6 us)
Async XLA Ops:
  7.2 91.5 %copy-start = (bf16[100,768]{1,0:T(8,128)(2,1)S(1)}, bf16[100,768]{1,0:T(8,128)(2,1)}, u32[]{:S(2)}) copy-start(bf16[100,768]{1,0:T(8,128)(2,1)} %param.33) | copy-start | bytes 460804
  7.2 88.8 %copy-start.36 = (bf16[768]{0:T(1024)(128)(2,1)S(1)}, bf16[768]{0:T(1024)(128)(2,1)}, u32[]{:S(2)}) copy-start(bf16[768]{0:T(1024)(128)(2,1)} %param.38) | copy-start | bytes 4612
  7.2 88.8 %copy-start.37 = (bf16[768]{0:T(1024)(128)(2,1)S(1)}, bf16[768]{0:T(1024)(128)(2,1)}, u32[]{:S(2)}) copy-start(bf16[768]{0:T(1024)(128)(2,1)} %param.39) | copy-start | bytes 4612
  7.2 88.8 %copy-start.46 = (s32[4]{0:T(128)S(1)}, s32[4]{0:T(128)}, u32[]{:S(2)}) copy-start(s32[4]{0:T(128)} %param.28) | copy-start | bytes 52
  7.2 89.0 %copy-start.38 = (bf16[768]{0:T(1024)(128)(2,1)S(1)}, bf16[768]{0:T(1024)(128)(2,1)}, u32[]{:S(2)}) copy-start(bf16[768]{0:T(1024)(128)(2,1)} %param.40) | copy-start | bytes 4612
  7.2 89.0 %copy-start.39 = (bf16[768]{0:T(1024)(128)(2,1)S(1)}, bf16[768]{0:T(1024)(128)(2,1)}, u32[]{:S(2)}) copy-start(bf16[768]{0:T(1024)(128)(2,1)} %param.41) | copy-start | bytes 4612
  7.3 89.0 %copy-start.40 = (bf16[768]{0:T(1024)(128)(2,1)S(1)}, bf16[768]{0:T(1024)(128)(2,1)}, u32[]{:S(2)}) copy-start(bf16[768]{0:T(1024)(128)(2,1)} %param.42) | copy-start | bytes 4612
  7.3 89.0 %copy-start.30 = (bf16[3072]{0:T(1024)(128)(2,1)S(1)}, bf16[3072]{0:T(1024)(128)(2,1)}, u32[]{:S(2)}) copy-start(bf16[3072]{0:T(1024)(128)(2,1)} %param.44) | copy-start | bytes 18436
  7.3 89.0 %copy-start.41 = (bf16[768]{0:T(1024)(128)(2,1)S(1)}, bf16[768]{0:T(1024)(128)(2,1)}, u32[]{:S(2)}) copy-start(bf16[768]{0:T(1024)(128)(2,1)} %param.46) | copy-start | bytes 4612
  7.3 89.6 %copy-start.42 = (bf16[768]{0:T(1024)(128)(2,1)S(1)}, bf16[768]{0:T(1024)(128)(2,1)}, u32[]{:S(2)}) copy-start(bf16[768]{0:T(1024)(128)(2,1)} %param.47) | copy-start | bytes 4612
  7.3 90.2 %copy-start.43 = (bf16[768]{0:T(1024)(128)(2,1)S(1)}, bf16[768]{0:T(1024)(128)(2,1)}, u32[]{:S(2)}) copy-start(bf16[768]{0:T(1024)(128)(2,1)} %param.48) | copy-start | bytes 4612
  7.3 91.4 %copy-start.44 = (s32[4]{0:T(128)S(1)}, s32[4]{0:T(128)}, u32[]{:S(2)}) copy-start(s32[4]{0:T(128)} %param.30) | copy-start | bytes 52
  7.3 98.0 %all-gather.14.cloned.1.call-start = ((), (), s32[]{:S(2)}) async-start(), calls=%async_computation.15 | async-start | bytes 1622016 | tf_op jit(solution)/shard_map/all_gather | solution.py:138
  8.1 122.7 %all-gather.18.cloned.1.call-start = ((), (), s32[]{:S(2)}) async-start(), calls=%async_computation.17 | async-start | bytes 1622016 | tf_op jit(solution)/shard_map/all_gather | solution.py:140
  8.8 174.5 %all-gather.16.cloned.1.call-start = ((), (), s32[]{:S(2)}) async-start(), calls=%async_computation.16 | async-start | bytes 1622016 | tf_op jit(solution)/shard_map/all_gather | solution.py:139
  9.5 459.9 %all-gather.20.cloned.1.call-start = ((), (), s32[]{:S(2)}) async-start(), calls=%async_computation.18 | async-start | bytes 1622016 | tf_op jit(solution)/shard_map/all_gather | solution.py:141
  10.1 474.1 %all-gather.22.cloned.1.call-start = ((), (), s32[]{:S(2)}) async-start(), calls=%async_computation.19 | async-start | bytes 4866048 | tf_op jit(solution)/shard_map/all_gather | solution.py:147
  10.7 482.7 %all-gather.24.cloned.1.call-start = ((), (), s32[]{:S(2)}) async-start(), calls=%async_computation.20 | async-start | bytes 4866048 | tf_op jit(solution)/shard_map/all_gather | solution.py:148
  11.3 1354.3 %all-reduce.3.cloned.1.call-start = ((), (), s32[]{:S(2)}) async-start(), calls=%async_computation.8 | async-start | bytes 638976 | tf_op jit(solution)/shard_map/psum | solution.py:323
  96.3 481.9 %copy-start.33 = (f32[768]{0:T(1024)}, f32[768]{0:T(1024)S(1)}, u32[]{:S(2)}) copy-start(f32[768]{0:T(1024)S(1)} %convert_element_type.204) | copy-start | bytes 9220
  464.3 5.1 copy-start.47
  473.0 7.5 copy-start.19
  484.1 9.2 copy-start.21
  501.5 6.7 slice-start.2
  509.4 68.8 %copy-start.35 = (f32[768]{0:T(1024)S(1)}, f32[768]{0:T(1024)}, u32[]{:S(2)}) copy-start(f32[768]{0:T(1024)} %convert_element_type.208) | copy-start | bytes 9220
  606.4 29.2 %copy-start.12 = (bf16[2048,768]{1,0:T(8,128)(2,1)}, bf16[2048,768]{1,0:T(8,128)(2,1)S(1)}, u32[]{:S(2)}) copy-start(bf16[2048,768]{1,0:T(8,128)(2,1)S(1)} %get-tuple-element.188) | copy-start | bytes 9437188
  635.7 19.3 copy-start.22
  659.2 6.1 copy-start.2
  1166.1 11.6 slice-start
  1167.1 5.0 copy-start.13
  1167.1 10.5 slice-start.1
  1172.2 5.5 copy-start.11
  1172.2 5.5 copy-start.29
  1177.6 9.7 copy-start.8
  1191.5 235.3 %reduce-scatter.16.cloned.1.call-start = ((), (), s32[]{:S(2)}) async-start(), calls=%async_computation.12 | async-start | bytes 3244032 | tf_op jit(solution)/shard_map/reduce_scatter | solution.py:300
  1199.5 369.2 %reduce-scatter.8.cloned.1.call-start = ((), (), s32[]{:S(2)}) async-start(), calls=%async_computation.7 | async-start | bytes 2162688 | tf_op jit(solution)/shard_map/reduce_scatter | solution.py:276
  1211.2 463.2 %reduce-scatter.10.cloned.1.call-start = ((), (), s32[]{:S(2)}) async-start(), calls=%async_computation.9 | async-start | bytes 3244032 | tf_op jit(solution)/shard_map/reduce_scatter | solution.py:282
  1228.8 552.9 %reduce-scatter.12.cloned.1.call-start = ((), (), s32[]{:S(2)}) async-start(), calls=%async_computation.10 | async-start | bytes 3244032 | tf_op jit(solution)/shard_map/reduce_scatter | solution.py:288
  1236.8 652.0 %reduce-scatter.14.cloned.1.call-start = ((), (), s32[]{:S(2)}) async-start(), calls=%async_computation.11 | async-start | bytes 3244032 | tf_op jit(solution)/shard_map/reduce_scatter | solution.py:294
  1244.8 785.6 %reduce-scatter.20.cloned.1.call-start = ((), (), s32[]{:S(2)}) async-start(), calls=%async_computation.14 | async-start | bytes 9732096 | tf_op jit(solution)/shard_map/reduce_scatter | solution.py:315
  1272.5 899.4 %reduce-scatter.18.cloned.1.call-start = ((), (), s32[]{:S(2)}) async-start(), calls=%async_computation.13 | async-start | bytes 9732096 | tf_op jit(solution)/shard_map/reduce_scatter | solution.py:309
  1313.5 11.3 copy-start.24
  1313.5 11.3 copy-start.25
  1313.6 11.3 copy-start.26
  1313.6 11.3 copy-start.28
  1313.6 11.3 copy-start.31
  1313.6 11.3 copy-start.32
  1313.6 860.0 %copy-start.1 = (bf16[100,768]{1,0:T(8,128)(2,1)S(1)}, bf16[100,768]{1,0:T(8,128)(2,1)}, u32[]{:S(2)}) copy-start(bf16[100,768]{1,0:T(8,128)(2,1)} %param.33) | copy-start | bytes 460804
  (19 other events, 54.0 us)
Sparse Core Ops, SparseCore 0:
  11.0 58.6 all-gather.13
  72.6 53.8 all-gather.17
  129.4 53.8 all-gather.15
  186.1 53.9 all-gather.19
  242.7 62.4 all-gather.21
  307.9 61.8 all-gather.23
  1191.6 125.9 all-reduce.2
  1323.6 103.1 reduce-scatter.15
  1429.6 139.1 reduce-scatter.7
  1574.6 99.7 reduce-scatter.9
  1680.4 101.1 reduce-scatter.11
  1787.5 101.1 reduce-scatter.13
  1895.2 135.1 reduce-scatter.19
  2036.7 135.1 reduce-scatter.17
where the time goes:
time: 2200 us; the launch traced here: 2180 us
  waiting for transfers between devices  837 us (38%)
  matrix products  730 us (33%)
  local copies, waits for them, and re-layouts  344 us (16%)
  other arithmetic  131 us (6%)
  blocking collectives  121 us (6%)
    dot_general x150, matrix products, matmul_second_t(): lax.dot_general(left_side, right_side, (((1,), (1,)), ((), ())), preferre...  262 us
    dot_general x102, matrix products, matmul_first_t(): lax.dot_general(left_side, right_side, (((0,), (0,)), ((), ())), preferre...  243 us
    dot_general x103, matrix products, matmul(): return jnp.dot(left_side, right_side, preferred_element_type=jnp.float32)  224 us
    reduce_scatter x1, waiting for transfers between devices, on_device(): lax.psum_scatter(disassemble(position_local, wide_count, narrow_count), (...  142 us
    reduce_scatter x1, waiting for transfers between devices, on_device(): lax.psum_scatter(disassemble(down_weight_grad, wide_count, narrow_count),...  142 us
    reduce_scatter x1, waiting for transfers between devices, on_device(): lax.psum_scatter(disassemble(up_weight_grad, wide_count, narrow_count), (...  141 us
    reduce_scatter x1, waiting for transfers between devices, on_device(): lax.psum_scatter(disassemble(key_weight_grad, wide_count, narrow_count),...  107 us
    reduce_scatter x1, waiting for transfers between devices, on_device(): lax.psum_scatter(disassemble(value_weight_grad, wide_count, narrow_count)...  107 us
  transfers between devices with their start and end apart: 14, of which 8 were waited for; matrix products, arithmetic and copies ran while one was open for 23% of the time, Pallas kernels for 0%

commit v1 on v0

--- a/solution.py
+++ b/solution.py
@@ -7,6 +7,18 @@
 H = 12
 HD = 64
 EPSILON = 1e-05
+
+
+def doubled_up(x, axis, dim):
+    ways, here = (lax.axis_size(axis), lax.axis_index(axis))
+    grown, reach = (x, 1)
+    while reach < ways:
+        theirs = lax.ppermute(grown, axis, [(d, d ^ reach) for d in range(ways)])
+        mine_first = jnp.concatenate([grown, theirs], axis=dim)
+        theirs_first = jnp.concatenate([theirs, grown], axis=dim)
+        grown = jnp.where(here & reach == 0, mine_first, theirs_first)
+        reach = 2 * reach
+    return grown
 
 
 def normalize(inputs, scales, offset):
@@ -134,7 +146,7 @@
     wide_count = lax.axis_size("wide")
     narrow_count = lax.axis_size("narrow")
     attention_stacks = (
-        lax.all_gather(position_table[None], ("wide", "narrow"), axis=0, tiled=True),
+        doubled_up(position_table[None], ("wide", "narrow"), 0),
         lax.all_gather(query_weight[None], ("wide", "narrow"), axis=0, tiled=True),
         lax.all_gather(key_weight[None], ("wide", "narrow"), axis=0, tiled=True),
         lax.all_gather(value_weight[None], ("wide", "narrow"), axis=0, tiled=True),

time: 2200 us -> 2200 us (level)
  blocking collectives: 121 us -> 40.6 us
  waiting for transfers between devices: 837 us -> 898 us
    all_gather x1 -> x0, blocking collectives: 79.9 us -> none  [on_device(): lax.all_gather(position_table[None], ('wide', 'narrow'), axis=0, tiled=True)]
    all_gather x1, waiting for transfers between devices: 0.01 us -> 31.4 us  [on_device(): lax.all_gather(value_weight[None], ('wide', 'narrow'), axis=0, tiled=True)]
  transfers between devices with their start and end apart: 14 -> 19, of which waited for: 8 -> 15; matrix products, arithmetic and copies ran while one was open for 23% -> 23% of each run, Pallas kernels for 0% -> 0%
where the time goes in v1:
time: 2200 us; the launch traced here: 2180 us
  waiting for transfers between devices  898 us (41%)
  matrix products  730 us (33%)
  local copies, waits for them, and re-layouts  344 us (16%)
  other arithmetic  139 us (6%)
  blocking collectives  40.6 us (2%)
    dot_general x150, matrix products, matmul_second_t(): lax.dot_general(left_side, right_side, (((1,), (1,)), ((), ())), preferre...  262 us
    dot_general x102, matrix products, matmul_first_t(): lax.dot_general(left_side, right_side, (((0,), (0,)), ((), ())), preferre...  243 us
    dot_general x103, matrix products, matmul(): return jnp.dot(left_side, right_side, preferred_element_type=jnp.float32)  224 us
    reduce_scatter x1, waiting for transfers between devices, on_device(): lax.psum_scatter(disassemble(position_local, wide_count, narrow_count), (...  142 us
    reduce_scatter x1, waiting for transfers between devices, on_device(): lax.psum_scatter(disassemble(down_weight_grad, wide_count, narrow_count),...  142 us
    reduce_scatter x1, waiting for transfers between devices, on_device(): lax.psum_scatter(disassemble(up_weight_grad, wide_count, narrow_count), (...  141 us
    reduce_scatter x1, waiting for transfers between devices, on_device(): lax.psum_scatter(disassemble(key_weight_grad, wide_count, narrow_count),...  107 us
    reduce_scatter x1, waiting for transfers between devices, on_device(): lax.psum_scatter(disassemble(value_weight_grad, wide_count, narrow_count)...  107 us
  transfers between devices with their start and end apart: 19, of which 15 were waited for; matrix products, arithmetic and copies ran while one was open for 23% of the time, Pallas kernels for 0%

profile of v1, /device:TPU:0, one launch (start us, length us, event | category | flops | bytes accessed | tf_op | source)
XLA Modules:
  0.0 2179.9 jit_solution(790534939612973937)
XLA Ops:
  25.6 6.5 collective-permute-done.3
  50.1 6.5 fusion.60
  56.5 12.3 all-gather.13.cloned.1.call-done
  73.2 6.2 add_convert_fusion.3
  86.5 7.7 copy.107
  94.2 31.4 %all-gather.17.cloned.1.call-done = bf16[3072,192]{1,0:T(8,128)(2,1)} async-done(((bf16[96,192]{1,0:T(8,128)(2,1)}), bf16[3072,192]{1,0:T(8,128)(2,1)}) %all-gather.17.cloned.1.call-update) | async-done | bytes 1179664 | tf_op jit(solution)/shard_map/all_gather | solution.py:152
  130.0 6.2 add_convert_fusion.2
  143.4 7.7 copy.109
  151.1 31.3 %all-gather.15.cloned.1.call-done = bf16[3072,192]{1,0:T(8,128)(2,1)} async-done(((bf16[96,192]{1,0:T(8,128)(2,1)}), bf16[3072,192]{1,0:T(8,128)(2,1)}) %all-gather.15.cloned.1.call-update) | async-done | bytes 1179664 | tf_op jit(solution)/shard_map/all_gather | solution.py:151
  187.0 6.2 convolution_convert_fusion.1
  200.3 7.7 copy.108
  208.4 255.0 %while.26 = (s32[]{:T(128)}, bf16[48,512,64]{1,2,0:T(8,128)(2,1)S(1)}, f32[48,512]{1,0:T(8,128)}, s32[48]{0:T(128)S(1)}, bf16[48,512,64]{2,1,0:T(8,128)(2,1)}, /...) while((s32[]{:T(128)}, bf16[48,512,64]{1,2,0:T(8,128)(2,1)S(1)}, ...), condition=%wide.region_3.4_spmd, body=%wide.region_0.3_spmd.sunk | while | flops 69206016 | bytes 3693681 | solution.py:193
  472.1 7.5 fusion.69
  483.2 6.0 copy.87
  492.4 8.2 reshape.357
  508.5 68.8 %multiply_convert_fusion.1 = (bf16[2048,3072]{1,0:T(8,128)(2,1)}, f32[2048,3072]{1,0:T(8,128)}, f32[2048,3072]{1,0:T(8,128)}) fusion(f32[3072]{0:T(1024)S(1)} %convert_element_type.206, bf16[768,3072]{1,0:T(8,128)(2,1)S(1)} %bitcast.363, f32[2048,768]{1,0:T(8,128)S(1)} %bitcast.332, f32[768]{0:T(1024)S(1)} %convert_element_type.204, ...), kind=kOutput, calls=%fused_computation.60 | convolution fusion | flops 10086776832 | bytes 73959424 | tf_op jit(solution)/shard_map/dot_general | solution.py:32
  577.3 15.1 fusion.70
  597.4 4.3 fusion.66
  605.5 29.2 %convert_reduce_fusion = (f32[3072]{0:T(1024)}, bf16[2048,3072]{1,0:T(8,128)(2,1)}) fusion(f32[2048,3072]{1,0:T(8,128)} %get-tuple-element.196, bf16[2048,768]{1,0:T(8,128)(2,1)S(1)} %get-tuple-element.188, bf16[3072,768]{0,1:T(8,128)(2,1)} %bitcast.365, f32[2048,3072]{1,0:T(8,128)} %get-tuple-element.209, f32[3072]{0:T(1024)S(1)} %convert_element_type.206), kind=kOutput, calls=%fused_computation.58 | convolution fusion | flops 9770628096 | bytes 70803456 | tf_op jit(solution)/shard_map/dot_general | solution.py:42
  634.8 19.2 multiply_reduce_fusion.1
  674.6 7.7 copy.112
  686.7 467.7 %while.27 = (s32[]{:T(128)}, bf16[48,512,64]{1,2,0:T(8,128)(2,1)S(1)}, bf16[48,512,64]{1,2,0:T(8,128)(2,1)}, bf16[48,512,64]{1,2,0:T(8,128)(2,1)}, s32[48]{0:T(1...) while((s32[]{:T(128)}, ...), condition=%wide.region_14.15_spmd, body=%wide.region_12.14_spmd.sunk | while | flops 170196992 | bytes 9191553 | solution.py:247
  1158.0 4.6 fusion.71
  1166.1 5.0 fusion.72
  1171.2 4.4 copy.97
  1176.7 9.6 select_reduce_fusion.1
  1190.5 8.0 fusion.76
  1198.6 4.6 reduce_sum.251
  1210.3 4.7 bitcast_convert_fusion
  1215.0 4.7 copy.99
  1219.7 8.0 fusion.73
  1227.8 7.9 fusion.74
  1235.8 8.0 fusion.75
  1243.9 16.4 fusion.77
  1260.3 5.9 copy.121
  1266.2 5.3 copy.103
  1272.2 18.5 fusion.61
  1290.7 12.7 reshape.371
  1303.4 9.1 copy.101
  1318.5 5.2 convert_reduce_fusion.4
  1323.9 40.6 %all-reduce = (f32[2,768]{1,0:T(2,128)}, f32[768]{0:T(1024)}, f32[768]{0:T(1024)}, f32[768]{0:T(1024)}, f32[768]{0:T(1024)}, /*index=5*/f32[768]{0:T(1024)}, f32...) all-reduce(f32[2,768]{1,0:T(2,128)S(1)} %pad_maximum_fusion, ...), channel_id=1, replica_groups=mesh['wide'=8,'narrow'=4] {'wide','narrow'}, use_global_device_ids=true, to_apply=%region_19.20 | all-reduce | flops 10752 | bytes 86016 | tf_op jit(solution)/shard_map/psum | solution.py:335
  1364.5 61.3 %reduce-scatter.16.cloned.1.call-done = f32[1,96,192]{2,1,0:T(8,128)} async-done(((f32[32,96,192]{2,1,0:T(8,128)}), f32[1,96,192]{2,1,0:T(8,128)}) %reduce-scatter.16.cloned.1.call-update) | async-done | bytes 73744 | tf_op jit(solution)/shard_map/reduce_scatter | solution.py:312
  1425.8 142.2 %reduce-scatter.8.cloned.1.call-done = f32[1,64,192]{2,1,0:T(8,128)} async-done(((f32[32,64,192]{2,1,0:T(8,128)}), f32[1,64,192]{2,1,0:T(8,128)}) %reduce-scatter.8.cloned.1.call-update) | async-done | bytes 49168 | tf_op jit(solution)/shard_map/reduce_scatter | solution.py:288
  1568.0 105.7 %reduce-scatter.10.cloned.1.call-done = f32[1,96,192]{2,1,0:T(8,128)} async-done(((f32[32,96,192]{2,1,0:T(8,128)}), f32[1,96,192]{2,1,0:T(8,128)}) %reduce-scatter.10.cloned.1.call-update) | async-done | bytes 73744 | tf_op jit(solution)/shard_map/reduce_scatter | solution.py:294
  1673.7 107.2 %reduce-scatter.12.cloned.1.call-done = f32[1,96,192]{2,1,0:T(8,128)} async-done(((f32[32,96,192]{2,1,0:T(8,128)}), f32[1,96,192]{2,1,0:T(8,128)}) %reduce-scatter.12.cloned.1.call-update) | async-done | bytes 73744 | tf_op jit(solution)/shard_map/reduce_scatter | solution.py:300
  1780.9 107.1 %reduce-scatter.14.cloned.1.call-done = f32[1,96,192]{2,1,0:T(8,128)} async-done(((f32[32,96,192]{2,1,0:T(8,128)}), f32[1,96,192]{2,1,0:T(8,128)}) %reduce-scatter.14.cloned.1.call-update) | async-done | bytes 73744 | tf_op jit(solution)/shard_map/reduce_scatter | solution.py:306
  1888.0 141.7 %reduce-scatter.20.cloned.1.call-done = f32[1,384,192]{1,2,0:T(8,128)} async-done(((f32[32,384,192]{1,2,0:T(8,128)}), f32[1,384,192]{1,2,0:T(8,128)}) %reduce-scatter.20.cloned.1.call-update) | async-done | bytes 294928 | tf_op jit(solution)/shard_map/reduce_scatter | solution.py:327
  2029.7 141.5 %reduce-scatter.18.cloned.1.call-done = f32[1,96,768]{2,1,0:T(8,128)} async-done(((f32[32,96,768]{2,1,0:T(8,128)}), f32[1,96,768]{2,1,0:T(8,128)}) %reduce-scatter.18.cloned.1.call-update) | async-done | bytes 294928 | tf_op jit(solution)/shard_map/reduce_scatter | solution.py:321
  (977 shorter events, 876.2 us)
Async XLA Ops:
  7.2 37.8 %copy-start = (bf16[100,768]{1,0:T(8,128)(2,1)S(1)}, bf16[100,768]{1,0:T(8,128)(2,1)}, u32[]{:S(2)}) copy-start(bf16[100,768]{1,0:T(8,128)(2,1)} %param.33) | copy-start | bytes 460804
  7.2 61.6 %all-gather.13.cloned.1.call-start = ((), (), s32[]{:S(2)}) async-start(), calls=%async_computation.15 | async-start | bytes 1622016 | tf_op jit(solution)/shard_map/all_gather | solution.py:150
  7.9 117.7 %all-gather.17.cloned.1.call-start = ((), (), s32[]{:S(2)}) async-start(), calls=%async_computation.17 | async-start | bytes 1622016 | tf_op jit(solution)/shard_map/all_gather | solution.py:152
  8.7 173.8 %all-gather.15.cloned.1.call-start = ((), (), s32[]{:S(2)}) async-start(), calls=%async_computation.16 | async-start | bytes 1622016 | tf_op jit(solution)/shard_map/all_gather | solution.py:151
  9.4 459.1 %all-gather.19.cloned.1.call-start = ((), (), s32[]{:S(2)}) async-start(), calls=%async_computation.18 | async-start | bytes 1622016 | tf_op jit(solution)/shard_map/all_gather | solution.py:153
  10.0 473.2 %all-gather.21.cloned.1.call-start = ((), (), s32[]{:S(2)}) async-start(), calls=%async_computation.19 | async-start | bytes 4866048 | tf_op jit(solution)/shard_map/all_gather | solution.py:159
  10.6 481.8 %all-gather.23.cloned.1.call-start = ((), (), s32[]{:S(2)}) async-start(), calls=%async_computation.20 | async-start | bytes 4866048 | tf_op jit(solution)/shard_map/all_gather | solution.py:160
  10.6 5.2 collective-permute-start
  16.7 5.3 collective-permute-start.1
  22.1 1.4 collective-permute-start.2
  23.6 8.5 collective-permute-start.3
  25.5 1339.0 %all-reduce.3.cloned.1.call-start = ((), (), s32[]{:S(2)}) async-start(), calls=%async_computation.8 | async-start | bytes 638976 | tf_op jit(solution)/shard_map/psum | solution.py:335
  32.3 14.0 collective-permute-start.4
  39.8 537.4 %copy-start.32 = (f32[768]{0:T(1024)}, f32[768]{0:T(1024)S(1)}, u32[]{:S(2)}) copy-start(f32[768]{0:T(1024)S(1)} %convert_element_type.204) | copy-start | bytes 9220
  463.4 5.1 copy-start.36
  472.1 7.5 copy-start.19
  483.2 9.2 copy-start.21
  500.6 6.7 slice-start.2
  503.7 3.6 copy-start.9
  503.7 4.8 slice-start.3
  508.5 68.8 %copy-start.34 = (f32[768]{0:T(1024)S(1)}, f32[768]{0:T(1024)}, u32[]{:S(2)}) copy-start(f32[768]{0:T(1024)} %convert_element_type.208) | copy-start | bytes 9220
  593.3 4.2 copy-start.27
  605.5 29.2 %copy-start.12 = (bf16[2048,768]{1,0:T(8,128)(2,1)}, bf16[2048,768]{1,0:T(8,128)(2,1)S(1)}, u32[]{:S(2)}) copy-start(bf16[2048,768]{1,0:T(8,128)(2,1)S(1)} %get-tuple-element.188) | copy-start | bytes 9437188
  634.8 19.2 copy-start.22
  658.2 6.1 copy-start.2
  682.3 4.4 copy-start.37
  1157.9 4.7 copy-start.14
  1157.9 4.6 copy-start.7
  1165.0 11.6 slice-start
  1166.1 5.1 copy-start.13
  1166.1 10.5 slice-start.1
  1171.2 5.5 copy-start.11
  1171.2 5.5 copy-start.29
  1176.6 9.7 copy-start.8
  1190.5 235.4 %reduce-scatter.16.cloned.1.call-start = ((), (), s32[]{:S(2)}) async-start(), calls=%async_computation.12 | async-start | bytes 3244032 | tf_op jit(solution)/shard_map/reduce_scatter | solution.py:312
  1198.5 369.4 %reduce-scatter.8.cloned.1.call-start = ((), (), s32[]{:S(2)}) async-start(), calls=%async_computation.7 | async-start | bytes 2162688 | tf_op jit(solution)/shard_map/reduce_scatter | solution.py:288
  1210.3 463.4 %reduce-scatter.10.cloned.1.call-start = ((), (), s32[]{:S(2)}) async-start(), calls=%async_computation.9 | async-start | bytes 3244032 | tf_op jit(solution)/shard_map/reduce_scatter | solution.py:294
  1227.8 553.1 %reduce-scatter.12.cloned.1.call-start = ((), (), s32[]{:S(2)}) async-start(), calls=%async_computation.10 | async-start | bytes 3244032 | tf_op jit(solution)/shard_map/reduce_scatter | solution.py:300
  1235.8 652.2 %reduce-scatter.14.cloned.1.call-start = ((), (), s32[]{:S(2)}) async-start(), calls=%async_computation.11 | async-start | bytes 3244032 | tf_op jit(solution)/shard_map/reduce_scatter | solution.py:306
  1243.8 785.9 %reduce-scatter.20.cloned.1.call-start = ((), (), s32[]{:S(2)}) async-start(), calls=%async_computation.14 | async-start | bytes 9732096 | tf_op jit(solution)/shard_map/reduce_scatter | solution.py:327
  1271.5 899.7 %reduce-scatter.18.cloned.1.call-start = ((), (), s32[]{:S(2)}) async-start(), calls=%async_computation.13 | async-start | bytes 9732096 | tf_op jit(solution)/shard_map/reduce_scatter | solution.py:321
  1312.5 11.3 copy-start.24
  1312.5 11.3 copy-start.25
  1312.5 11.3 copy-start.26
  1312.5 11.3 copy-start.28
  1312.5 11.3 copy-start.30
  1312.6 11.3 copy-start.31
  1312.6 860.3 %copy-start.1 = (bf16[100,768]{1,0:T(8,128)(2,1)S(1)}, bf16[100,768]{1,0:T(8,128)(2,1)}, u32[]{:S(2)}) copy-start(bf16[100,768]{1,0:T(8,128)(2,1)} %param.33) | copy-start | bytes 460804
  (13 other events, 27.7 us)
Sparse Core Ops, SparseCore 0:
  10.9 57.8 all-gather.12
  71.7 53.8 all-gather.16
  128.5 53.8 all-gather.14
  185.2 53.9 all-gather.18
  241.8 62.4 all-gather.20
  307.0 62.0 all-gather.22
  1190.6 126.0 all-reduce.2
  1322.7 103.1 reduce-scatter.15
  1428.7 139.2 reduce-scatter.7
  1573.8 99.8 reduce-scatter.9
  1679.7 101.1 reduce-scatter.11
  1786.8 101.1 reduce-scatter.13
  1894.5 135.1 reduce-scatter.19
  2036.0 135.1 reduce-scatter.17
